TPU v7x, 32 devices: a whole 2x2x4 slice. The times are simulated.
32 devices in a mesh: crop: 4 (over z), scene: 8 (over y, x, core).
Axes of the slice: x: 2, y: 2, z: 4, core: 2. Of those that a mesh axis runs over, the one named last changes fastest.
Arguments:
- fine_feats: bfloat16 [4, 49152, 128], P('crop', 'scene'), may hold values from -6 to 6
- out_grad: bfloat16 [4, 49152, 128], P('crop', 'scene'), may hold values from -6 to 6
- pre_act: bfloat16 [4, 8, 8, 8, 64, 256], P('crop', 'scene'), may hold values from -6 to 6
- deep_grad: bfloat16 [4, 8, 8, 8, 64, 256], P('crop', 'scene'), may hold values from -6 to 6
- down_weight: bfloat16 [8, 128, 256], replicated, may hold values from -0.3125 to 0.3125
- up_weight: bfloat16 [8, 256, 128], replicated, may hold values from -0.375 to 0.375
- block_owner: int32 [4, 256, 1], P('crop', 'scene'), may hold values from 0 to 7; in each aligned block of 32 rows (0 to 31, 32 to 63, ..., all dimensions but the last counted through in order) at most 8 rows name the same one
- parent_slot: int32 [4, 49152], P('crop', 'scene'), may hold values from 0 to 63, as said below
- child_offset: int32 [4, 49152], P('crop', 'scene'), may hold values from 0 to 7, as said below
Outputs:
- fine_grad: bfloat16 [4, 49152, 128], P('crop', 'scene')
- down_grad: float32 [8, 128, 256], replicated
- up_grad: float32 [8, 256, 128], replicated
- bias_grad: float32 [256], replicated
Inputs may be any that keep to these rules, and one draw needn't show every extreme that they name: `parent_slot`: within each aligned block of 192 fine sites the parent index never falls and each of the 64 parents has 1 to 8 sites. `child_offset`: offsets strictly rise within one parent. `block_owner`: among the 32 blocks of one scene index no owner is named more than 8 times, a bound that some block reaches.
All inputs are finite; a program needn't handle non-finite values.
Results may differ from a plain program's by a relative error of at most 0.005.
Values may be sent and summed in bfloat16 or wider, within the bound.
No kernel may reach another device: no remote copies, remote signals or barrier semaphores. Data moves between devices by JAX's collectives and lax.ppermute only.
A program may use at most 128 MiB of HBM per device.

v0:
```python
import jax
import jax.numpy as jnp
from jax import lax
from jax.sharding import PartitionSpec as P


def silu_parts(pre_value):
    pre_float = pre_value.astype(jnp.float32)
    sig_value = jax.nn.sigmoid(pre_float)
    return (pre_float * sig_value, sig_value * (1.0 + pre_float * (1.0 - sig_value)))


def pick_rows(row_ids, total_rows, table):
    selector = (row_ids[:, None] == jnp.arange(total_rows, dtype=jnp.int32)[None, :]).astype(
        table.dtype
    )
    picked = jnp.dot(selector, table.reshape(total_rows, -1), preferred_element_type=jnp.float32)
    return picked.astype(table.dtype).reshape((row_ids.shape[0],) + table.shape[1:])


def local_grads(feats, cotan, places, parent_pre, parent_deep, wu_mat, wd_mat):
    block_total, rows_block, width = feats.shape
    parents_block = parent_pre.shape[1]
    out_width = parent_pre.shape[2]
    slot_ids = jnp.arange(parents_block * 8, dtype=jnp.int32)
    chooser = (places[:, :, None] == slot_ids[None, None, :]).astype(jnp.bfloat16)
    feat_slots = (
        jnp.einsum("brs,brc->bsc", chooser, feats, preferred_element_type=jnp.float32)
        .astype(feats.dtype)
        .reshape(-1, 8 * width)
    )
    cot_slots = (
        jnp.einsum("brs,brc->bsc", chooser, cotan, preferred_element_type=jnp.float32)
        .astype(cotan.dtype)
        .reshape(-1, 8 * width)
    )
    act_value, slope_value = silu_parts(parent_pre.reshape(-1, out_width))
    act_grad = parent_deep.reshape(-1, out_width).astype(jnp.float32) + jnp.dot(
        cot_slots, wu_mat, preferred_element_type=jnp.float32
    )
    pre_grad = act_grad * slope_value
    pre_grad = pre_grad.astype(jnp.bfloat16)
    slot_grads = jnp.dot(pre_grad, wd_mat, preferred_element_type=jnp.float32).astype(jnp.bfloat16)
    slot_grads = slot_grads.reshape(block_total, parents_block * 8, width)
    fine_part = jnp.einsum(
        "brs,bsc->brc", chooser, slot_grads, preferred_element_type=jnp.float32
    ).astype(jnp.bfloat16)
    contract = (((0,), (0,)), ((), ()))
    up_term = lax.dot_general(
        act_value.astype(jnp.bfloat16), cot_slots, contract, preferred_element_type=jnp.float32
    )
    down_term = lax.dot_general(feat_slots, pre_grad, contract, preferred_element_type=jnp.float32)
    bias_term = jnp.sum(pre_grad.astype(jnp.float32), axis=0)
    return (fine_part, up_term, down_term, bias_term)


def on_device(
    fine_feats,
    out_grad,
    pre_act,
    deep_grad,
    down_weight,
    up_weight,
    block_owner,
    parent_slot,
    child_offset,
):
    scene_count = lax.axis_size("scene")
    crop_count = lax.axis_size("crop")
    width = fine_feats.shape[2]
    out_width = pre_act.shape[5]
    capacity = pre_act.shape[3]
    parents_block = pre_act.shape[4]
    owners = block_owner[0, :, 0]
    block_count = owners.shape[0]
    rows_block = fine_feats.shape[1] // block_count
    wu_mat = jnp.transpose(up_weight, (0, 2, 1)).reshape(8 * width, out_width)
    wd_mat = jnp.transpose(down_weight, (2, 0, 1)).reshape(out_width, 8 * width)
    earlier = jnp.arange(block_count)[None, :] < jnp.arange(block_count)[:, None]
    same_owner = owners[:, None] == owners[None, :]
    slot_rank = jnp.sum(same_owner & earlier, axis=1)
    target = owners * capacity + slot_rank
    places = (parent_slot[0] * 8 + child_offset[0]).reshape(block_count, rows_block)
    feats = fine_feats[0].reshape(block_count, rows_block, width)
    cotan = out_grad[0].reshape(block_count, rows_block, width)
    slot_total = scene_count * capacity
    pre_here, deep_here = (
        lax.all_to_all(pre_act[0, 0], "scene", split_axis=0, concat_axis=0, tiled=True),
        lax.all_to_all(deep_grad[0, 0], "scene", split_axis=0, concat_axis=0, tiled=True),
    )
    pre_blocks = pick_rows(
        target, slot_total, pre_here.reshape(slot_total, parents_block, out_width)
    )
    deep_blocks = pick_rows(
        target, slot_total, deep_here.reshape(slot_total, parents_block, out_width)
    )
    fine_part, up_term, down_term, bias_term = local_grads(
        feats, cotan, places, pre_blocks, deep_blocks, wu_mat, wd_mat
    )
    up_total, down_total, bias_total = lax.psum((up_term, down_term, bias_term), ("crop", "scene"))
    grad_scale = float(crop_count * scene_count * fine_feats.shape[1]) ** (-0.5)
    up_grad = jnp.transpose((up_total * grad_scale).reshape(out_width, 8, width), (1, 0, 2))
    down_grad = (down_total * grad_scale).reshape(8, width, out_width)
    return (fine_part.reshape(1, -1, width), down_grad, up_grad, bias_total * grad_scale)


def solution(mesh):
    return jax.shard_map(
        on_device,
        mesh=mesh,
        in_specs=(
            P("crop", "scene", None),
            P("crop", "scene", None),
            P("crop", "scene", None, None, None, None),
            P("crop", "scene", None, None, None, None),
            P(),
            P(),
            P("crop", "scene", None),
            P("crop", "scene"),
            P("crop", "scene"),
        ),
        out_specs=(P("crop", "scene", None), P(), P(), P()),
        check_vma=False,
    )
```

profile of v0, /device:TPU:0, one launch (start us, length us, event | category | flops | bytes accessed | tf_op | source)
XLA Modules:
  0.0 248.8 jit_solution(13823868329120480726)
XLA Ops:
  7.2 0.0 copy-start
  7.2 32.0 %all_to_all.10 = bf16[8,8,64,256]{3,2,1,0:T(8,128)(2,1)} all-to-all(bf16[8,8,64,256]{3,2,1,0:T(8,128)(2,1)} %bitcast.42), channel_id=1, replica_groups=mesh['crop'=4,'scene'=8] {'scene'}, dimensions={0} | all-to-all | bytes 4194304 | tf_op jit(solution)/shard_map/all_to_all | solution.py:88
  39.2 4.5 %all-to-all-start = ((bf16[8,8,64,256]{3,2,1,0:T(8,128)(2,1)}), bf16[8,8,64,256]{3,2,1,0:T(8,128)(2,1)}, u32[]{:S(2)}, u32[]{:S(2)}) async-start(bf16[8,8,64,256]{3,2,1,0:T(8,128)(2,1)} %bitcast.43), calls=%async_computation | async-start | bytes 4194304 | tf_op jit(solution)/shard_map/all_to_all | solution.py:89
  43.7 0.0 all-reduce.3.cloned.1.call-start
  43.8 0.1 add_reduce_fusion
  43.8 0.1 add.36
  43.9 7.1 %fusion.8 = bf16[32,512,128]{2,1,0:T(8,128)(2,1)} fusion(bf16[32,192,128]{2,1,0:T(8,128)(2,1)S(1)} %bitcast.40, s32[32,192]{1,0:T(8,128)S(1)} %add.36), kind=kOutput, calls=%fused_computation.12 | convolution fusion | flops 810549248 | bytes 5791744 | tf_op jit(solution)/shard_map/brs,brc->bsc/dot_general | solution.py:33
  51.0 7.3 %reshape.60 = bf16[2048,1024]{1,0:T(8,128)(2,1)} reshape(bf16[32,512,128]{2,1,0:T(8,128)(2,1)} %fusion.8) | data formatting | bytes 8388608 | tf_op jit(solution)/shard_map/reshape | solution.py:35
  58.4 0.2 copy.16
  58.6 8.1 %fusion.9 = bf16[32,512,128]{2,1,0:T(8,128)(2,1)} fusion(bf16[32,192,128]{2,1,0:T(8,128)(2,1)} %bitcast.48, s32[32,192]{1,0:T(8,128)S(1)} %add.36), kind=kOutput, calls=%fused_computation.13 | convolution fusion | flops 810549248 | bytes 5791744 | tf_op jit(solution)/shard_map/brs,brc->bsc/dot_general | solution.py:28
  66.7 7.3 %reshape.65 = bf16[2048,1024]{1,0:T(8,128)(2,1)} reshape(bf16[32,512,128]{2,1,0:T(8,128)(2,1)} %fusion.9) | data formatting | bytes 8388608 | tf_op jit(solution)/shard_map/reshape | solution.py:30
  74.0 0.2 convert_reduce_fusion.1
  74.2 2.9 %copy.20 = bf16[8,8,64,256]{3,1,2,0:T(8,128)(2,1)S(1)} copy(bf16[8,8,64,256]{3,2,1,0:T(8,128)(2,1)} %all_to_all.10) | data formatting | bytes 4194304
  77.1 2.0 multiply_convert_fusion
  79.1 2.7 %reshape.69 = f32[2048,256]{1,0:T(8,128)} reshape(f32[32,16384]{1,0:T(8,128)} %get-tuple-element.7) | data formatting | bytes 4194304 | tf_op jit(solution)/shard_map/convert_element_type | solution.py:8
  81.9 2.9 %copy.19 = bf16[8,8,64,256]{3,1,2,0:T(8,128)(2,1)S(1)} copy(bf16[8,8,64,256]{3,2,1,0:T(8,128)(2,1)} %all-to-all-done) | data formatting | bytes 4194304
  84.7 1.8 fusion.1
  86.6 2.7 %reshape.68 = f32[2048,256]{1,0:T(8,128)} reshape(f32[32,16384]{1,0:T(8,128)} %fusion.1) | data formatting | bytes 4194304 | tf_op jit(solution)/shard_map/convert_element_type | solution.py:38
  89.3 1.3 convert_element_type.65
  90.6 4.9 %fusion.17 = f32[256,1024]{1,0:T(8,128)} fusion(bf16[2048,256]{1,0:T(8,128)(2,1)} %convert_element_type.65, bf16[2048,1024]{1,0:T(8,128)(2,1)} %reshape.60), kind=kOutput, calls=%fused_computation.33 | convolution fusion | flops 1073741824 | bytes 6291456 | tf_op jit(solution)/shard_map/dot_general | solution.py:49
  95.5 3.5 %convert_reduce_fusion = (f32[256]{0:T(256)S(1)}, bf16[2048,256]{1,0:T(8,128)(2,1)S(1)}) fusion(f32[2048,256]{1,0:T(8,128)S(1)} %copy-done.3, f32[2048,256]{1,0:T(8,128)} %reshape.68, bf16[2048,1024]{1,0:T(8,128)(2,1)S(1)} %copy-done.2, bf16[1024,256]{1,0:T(8,128)(2,1)S(1)} %bitcast.47), kind=kOutput, calls=%fused_computation.17 | convolution fusion | flops 1080033024 | bytes 9962496 | tf_op jit(solution)/shard_map/dot_general | solution.py:38
  99.0 2.3 fusion.16
  101.3 0.0 all-reduce.3.cloned.1.call-update
  101.3 1.0 copy-done.5
  102.3 3.2 %convolution_convert_fusion.2 = bf16[2048,1024]{1,0:T(8,128)(2,1)} fusion(bf16[2048,256]{1,0:T(8,128)(2,1)S(1)} %get-tuple-element.9, bf16[256,1024]{0,1:T(8,128)(2,1)S(1)} %bitcast.46), kind=kOutput, calls=%fused_computation.11 | convolution fusion | flops 1075838976 | bytes 5767168 | tf_op jit(solution)/shard_map/dot_general | solution.py:43
  105.6 7.4 %reshape.63 = bf16[32,512,128]{2,1,0:T(8,128)(2,1)} reshape(bf16[2048,1024]{1,0:T(8,128)(2,1)} %convolution_convert_fusion.2) | data formatting | bytes 8388608 | tf_op jit(solution)/shard_map/reshape | solution.py:44
  112.9 41.4 %psum.23 = f32[256]{0:T(256)S(1)} all-reduce(f32[256]{0:T(256)S(1)} %get-tuple-element.8), channel_id=1, replica_groups=mesh['crop'=4,'scene'=8] {'crop','scene'}, use_global_device_ids=true, to_apply=%region_4.0 | all-reduce | flops 256 | bytes 2048 | tf_op jit(solution)/shard_map/psum | solution.py:100
  154.3 0.6 broadcast_multiply_fusion.1
  154.9 4.9 %fusion.12 = bf16[32,192,128]{2,1,0:T(8,128)(2,1)} fusion(bf16[32,512,128]{2,1,0:T(8,128)(2,1)} %reshape.63, s32[32,192]{1,0:T(8,128)S(1)} %add.36), kind=kOutput, calls=%fused_computation.19 | convolution fusion | flops 809238528 | bytes 5791744 | tf_op jit(solution)/shard_map/brs,bsc->brc/dot_general | solution.py:45
  159.8 78.7 %all-reduce.3.cloned.1.call-done = (f32[1024,256]{1,0:T(8,128)}, f32[256,1024]{1,0:T(8,128)}) async-done(((f32[1024,256]{1,0:T(8,128)}, f32[256,1024]{1,0:T(8,128)}), (f32[1024,256]{1,0:T(8,128)}, f32[256,1024]{1,0:T(8,128)})) %all-reduce.3.cloned.1.call-update) | async-done | bytes 2097168 | tf_op jit(solution)/shard_map/psum | solution.py:100
  238.5 2.4 broadcast_multiply_fusion
  240.9 1.1 bitcast_bitcast_fusion
  (20 shorter events, 0.0 us)
Async XLA Ops:
  7.2 36.8 %copy-start = (bf16[1,6144,128]{2,1,0:T(8,128)(2,1)S(1)}, bf16[1,6144,128]{2,1,0:T(8,128)(2,1)}, u32[]{:S(2)}) copy-start(bf16[1,6144,128]{2,1,0:T(8,128)(2,1)} %param.10) | copy-start | bytes 4718596
  39.2 4.6 %copy-start.7 = (s32[1,6144]{1,0:T(1,128)S(1)}, s32[1,6144]{1,0:T(1,128)}, u32[]{:S(2)}) copy-start(s32[1,6144]{1,0:T(1,128)} %param.17) | copy-start | bytes 73732
  39.2 4.6 %copy-start.8 = (s32[1,6144]{1,0:T(1,128)S(1)}, s32[1,6144]{1,0:T(1,128)}, u32[]{:S(2)}) copy-start(s32[1,6144]{1,0:T(1,128)} %param.16) | copy-start | bytes 73732
  39.2 42.7 %all-to-all-start = ((bf16[8,8,64,256]{3,2,1,0:T(8,128)(2,1)}), bf16[8,8,64,256]{3,2,1,0:T(8,128)(2,1)}, u32[]{:S(2)}, u32[]{:S(2)}) async-start(bf16[8,8,64,256]{3,2,1,0:T(8,128)(2,1)} %bitcast.43), calls=%async_computation | async-start | bytes 4194304 | tf_op jit(solution)/shard_map/all_to_all | solution.py:89
  43.7 194.8 %all-reduce.3.cloned.1.call-start = ((), (), s32[]{:S(2)}) async-start(), calls=%async_computation.2 | async-start | bytes 4194304 | tf_op jit(solution)/shard_map/psum | solution.py:100
  51.0 7.3 %copy-start.6 = (bf16[8,256,128]{2,1,0:T(8,128)(2,1)S(1)}, bf16[8,256,128]{2,1,0:T(8,128)(2,1)}, u32[]{:S(2)}) copy-start(bf16[8,256,128]{2,1,0:T(8,128)(2,1)} %param.14) | copy-start | bytes 1572868
  66.7 7.3 %copy-start.9 = (s32[1,32,1]{1,2,0:T(1,128)S(1)}, s32[1,32,1]{1,2,0:T(1,128)}, u32[]{:S(2)}) copy-start(s32[1,32,1]{1,2,0:T(1,128)} %param.15) | copy-start | bytes 388
  90.6 4.9 %copy-start.2 = (bf16[2048,1024]{1,0:T(8,128)(2,1)S(1)}, bf16[2048,1024]{1,0:T(8,128)(2,1)}, u32[]{:S(2)}) copy-start(bf16[2048,1024]{1,0:T(8,128)(2,1)} %reshape.60) | copy-start | bytes 12582916
  90.6 4.9 %copy-start.3 = (f32[2048,256]{1,0:T(8,128)S(1)}, f32[2048,256]{1,0:T(8,128)}, u32[]{:S(2)}) copy-start(f32[2048,256]{1,0:T(8,128)} %reshape.69) | copy-start | bytes 6291460
  95.5 3.6 %copy-start.1 = (bf16[2048,1024]{1,0:T(8,128)(2,1)S(1)}, bf16[2048,1024]{1,0:T(8,128)(2,1)}, u32[]{:S(2)}) copy-start(bf16[2048,1024]{1,0:T(8,128)(2,1)} %reshape.65) | copy-start | bytes 12582916
  101.3 1.0 copy-start.5
  238.5 2.4 copy-start.4
Sparse Core Ops, SparseCore 0:
  101.5 136.9 all-reduce.2
where the time goes:
time: 250 us; the launch traced here: 249 us
  waiting for transfers between devices  78.7 us (31%)
  blocking collectives  73.4 us (29%)
  matrix products  37.9 us (15%)
  local copies, waits for them, and re-layouts  35.8 us (14%)
  between operations  14.1 us (6%)
  starting transfers between devices  4.54 us (2%)
  other arithmetic  4.26 us (2%)
    psum x1, waiting for transfers between devices, on_device(): lax.psum((up_term, down_term, bias_term), ('crop', 'scene'))  78.7 us
    psum x1, blocking collectives, on_device(): lax.psum((up_term, down_term, bias_term), ('crop', 'scene'))  41.4 us
    all_to_all x1, blocking collectives, on_device(): lax.all_to_all(pre_act[0, 0], 'scene', split_axis=0, concat_axis=0, tiled...  32 us
    dot_general x1, matrix products, local_grads(): jnp.einsum('brs,brc->bsc', chooser, feats, preferred_element_type=jnp.flo...  8.09 us
    reshape x1, local copies, waits for them, and re-layouts, local_grads(): slot_grads = slot_grads.reshape(block_total, parents_block * 8, width)  7.36 us
    reshape x1, local copies, waits for them, and re-layouts, local_grads(): cot_slots = jnp.einsum('brs,brc->bsc', chooser, cotan, preferred_element_...  7.34 us
    reshape x1, local copies, waits for them, and re-layouts, local_grads(): feat_slots = jnp.einsum('brs,brc->bsc', chooser, feats, preferred_element...  7.34 us
    dot_general x1, matrix products, local_grads(): jnp.einsum('brs,brc->bsc', chooser, cotan, preferred_element_type=jnp.flo...  7.12 us
  transfers between devices with their start and end apart: 2, of which 1 were waited for; matrix products, arithmetic and copies ran while one was open for 22% of the time, Pallas kernels for 0%

commit v1 on v0

--- a/solution.py
+++ b/solution.py
@@ -97,7 +97,9 @@
     fine_part, up_term, down_term, bias_term = local_grads(
         feats, cotan, places, pre_blocks, deep_blocks, wu_mat, wd_mat
     )
-    up_total, down_total, bias_total = lax.psum((up_term, down_term, bias_term), ("crop", "scene"))
+    up_total, down_total, bias_total = lax.psum(
+        lax.psum((up_term, down_term, bias_term), "scene"), "crop"
+    )
     grad_scale = float(crop_count * scene_count * fine_feats.shape[1]) ** (-0.5)
     up_grad = jnp.transpose((up_total * grad_scale).reshape(out_width, 8, width), (1, 0, 2))
     down_grad = (down_total * grad_scale).reshape(8, width, out_width)

time: 250 us -> 265 us (1.060)
  waiting for transfers between devices: 78.7 us -> 111 us
  blocking collectives: 73.4 us -> 56.9 us
    psum x1 -> x2, waiting for transfers between devices: 78.7 us -> 111 us  [the longest x1 64 us: on_device(): lax.psum((up_term, down_term, bias_term), 'scene')]
    psum x1 -> x2, blocking collectives: 41.4 us -> 24.9 us  [the longest x1 12.6 us: on_device(): lax.psum((up_term, down_term, bias_term), 'scene')]
  transfers between devices with their start and end apart: 2 -> 3, of which waited for: 1 -> 2; matrix products, arithmetic and copies ran while one was open for 22% -> 21% of each run, Pallas kernels for 0% -> 0%
where the time goes in v1:
time: 265 us; the launch traced here: 264 us
  waiting for transfers between devices  111 us (42%)
  blocking collectives  56.9 us (21%)
  matrix products  38 us (14%)
  local copies, waits for them, and re-layouts  34.9 us (13%)
  between operations  14.1 us (5%)
  starting transfers between devices  4.57 us (2%)
  other arithmetic  4.26 us (2%)
    psum x1, waiting for transfers between devices, on_device(): lax.psum((up_term, down_term, bias_term), 'scene')  64 us
    psum x1, waiting for transfers between devices, on_device(): lax.psum(lax.psum((up_term, down_term, bias_term), 'scene'), 'crop')  46.8 us
    all_to_all x1, blocking collectives, on_device(): lax.all_to_all(pre_act[0, 0], 'scene', split_axis=0, concat_axis=0, tiled...  32 us
    psum x1, blocking collectives, on_device(): lax.psum((up_term, down_term, bias_term), 'scene')  12.6 us
    psum x1, blocking collectives, on_device(): lax.psum(lax.psum((up_term, down_term, bias_term), 'scene'), 'crop')  12.3 us
    dot_general x1, matrix products, local_grads(): jnp.einsum('brs,brc->bsc', chooser, feats, preferred_element_type=jnp.flo...  8.09 us
    reshape x1, local copies, waits for them, and re-layouts, local_grads(): slot_grads = slot_grads.reshape(block_total, parents_block * 8, width)  7.39 us
    reshape x1, local copies, waits for them, and re-layouts, local_grads(): feat_slots = jnp.einsum('brs,brc->bsc', chooser, feats, preferred_element...  7.35 us
  transfers between devices with their start and end apart: 3, of which 2 were waited for; matrix products, arithmetic and copies ran while one was open for 21% of the time, Pallas kernels for 0%

profile of v1, /device:TPU:0, one launch (start us, length us, event | category | flops | bytes accessed | tf_op | source)
XLA Modules:
  0.0 263.6 jit_solution(17374839418193686651)
XLA Ops:
  7.2 32.0 %all_to_all.10 = bf16[8,8,64,256]{3,2,1,0:T(8,128)(2,1)} all-to-all(bf16[8,8,64,256]{3,2,1,0:T(8,128)(2,1)} %bitcast.42), channel_id=1, replica_groups=mesh['crop'=4,'scene'=8] {'scene'}, dimensions={0} | all-to-all | bytes 4194304 | tf_op jit(solution)/shard_map/all_to_all | solution.py:88
  39.2 4.5 %all-to-all-start = ((bf16[8,8,64,256]{3,2,1,0:T(8,128)(2,1)}), bf16[8,8,64,256]{3,2,1,0:T(8,128)(2,1)}, u32[]{:S(2)}, u32[]{:S(2)}) async-start(bf16[8,8,64,256]{3,2,1,0:T(8,128)(2,1)} %bitcast.43), calls=%async_computation | async-start | bytes 4194304 | tf_op jit(solution)/shard_map/all_to_all | solution.py:89
  43.7 0.0 all-reduce.5.cloned.1.call-start
  43.8 0.1 add_reduce_fusion
  43.8 0.1 add.42
  43.9 7.1 %fusion.8 = bf16[32,512,128]{2,1,0:T(8,128)(2,1)} fusion(bf16[32,192,128]{2,1,0:T(8,128)(2,1)S(1)} %bitcast.40, s32[32,192]{1,0:T(8,128)S(1)} %add.42), kind=kOutput, calls=%fused_computation.12 | convolution fusion | flops 810549248 | bytes 5791744 | tf_op jit(solution)/shard_map/brs,brc->bsc/dot_general | solution.py:33
  51.1 7.3 %reshape.60 = bf16[2048,1024]{1,0:T(8,128)(2,1)} reshape(bf16[32,512,128]{2,1,0:T(8,128)(2,1)} %fusion.8) | data formatting | bytes 8388608 | tf_op jit(solution)/shard_map/reshape | solution.py:35
  58.4 0.2 copy.16
  58.6 8.1 %fusion.9 = bf16[32,512,128]{2,1,0:T(8,128)(2,1)} fusion(bf16[32,192,128]{2,1,0:T(8,128)(2,1)} %bitcast.48, s32[32,192]{1,0:T(8,128)S(1)} %add.42), kind=kOutput, calls=%fused_computation.13 | convolution fusion | flops 810549248 | bytes 5791744 | tf_op jit(solution)/shard_map/brs,brc->bsc/dot_general | solution.py:28
  66.7 7.4 %reshape.65 = bf16[2048,1024]{1,0:T(8,128)(2,1)} reshape(bf16[32,512,128]{2,1,0:T(8,128)(2,1)} %fusion.9) | data formatting | bytes 8388608 | tf_op jit(solution)/shard_map/reshape | solution.py:30
  74.1 0.2 convert_reduce_fusion.1
  74.3 2.9 %copy.20 = bf16[8,8,64,256]{3,1,2,0:T(8,128)(2,1)S(1)} copy(bf16[8,8,64,256]{3,2,1,0:T(8,128)(2,1)} %all_to_all.10) | data formatting | bytes 4194304
  77.1 2.0 multiply_convert_fusion
  79.2 2.7 %reshape.69 = f32[2048,256]{1,0:T(8,128)} reshape(f32[32,16384]{1,0:T(8,128)} %get-tuple-element.9) | data formatting | bytes 4194304 | tf_op jit(solution)/shard_map/convert_element_type | solution.py:8
  81.9 2.9 %copy.19 = bf16[8,8,64,256]{3,1,2,0:T(8,128)(2,1)S(1)} copy(bf16[8,8,64,256]{3,2,1,0:T(8,128)(2,1)} %all-to-all-done) | data formatting | bytes 4194304
  84.8 1.8 fusion.1
  86.6 2.7 %reshape.68 = f32[2048,256]{1,0:T(8,128)} reshape(f32[32,16384]{1,0:T(8,128)} %fusion.1) | data formatting | bytes 4194304 | tf_op jit(solution)/shard_map/convert_element_type | solution.py:38
  89.3 1.3 convert_element_type.65
  90.6 4.9 %fusion.17 = f32[256,1024]{1,0:T(8,128)} fusion(bf16[2048,256]{1,0:T(8,128)(2,1)} %convert_element_type.65, bf16[2048,1024]{1,0:T(8,128)(2,1)} %reshape.60), kind=kOutput, calls=%fused_computation.33 | convolution fusion | flops 1073741824 | bytes 6291456 | tf_op jit(solution)/shard_map/dot_general | solution.py:49
  95.5 3.5 %convert_reduce_fusion = (f32[256]{0:T(256)S(1)}, bf16[2048,256]{1,0:T(8,128)(2,1)S(1)}) fusion(f32[2048,256]{1,0:T(8,128)S(1)} %copy-done.3, f32[2048,256]{1,0:T(8,128)} %reshape.68, bf16[2048,1024]{1,0:T(8,128)(2,1)S(1)} %copy-done.2, bf16[1024,256]{1,0:T(8,128)(2,1)S(1)} %bitcast.47), kind=kOutput, calls=%fused_computation.17 | convolution fusion | flops 1080033024 | bytes 9962496 | tf_op jit(solution)/shard_map/dot_general | solution.py:38
  99.0 2.3 fusion.16
  101.3 0.0 all-reduce.7.cloned.1.call-start
  101.4 64.0 %all-reduce.5.cloned.1.call-done = (f32[1024,256]{1,0:T(8,128)}, f32[256,1024]{1,0:T(8,128)}) async-done(((f32[1024,256]{1,0:T(8,128)}, f32[256,1024]{1,0:T(8,128)}), (f32[1024,256]{1,0:T(8,128)}, f32[256,1024]{1,0:T(8,128)})) %all-reduce.5.cloned.1.call-update) | async-done | bytes 2097168 | tf_op jit(solution)/shard_map/psum | solution.py:101
  165.5 3.2 %convolution_convert_fusion.2 = bf16[2048,1024]{1,0:T(8,128)(2,1)} fusion(bf16[2048,256]{1,0:T(8,128)(2,1)S(1)} %get-tuple-element.11, bf16[256,1024]{0,1:T(8,128)(2,1)S(1)} %bitcast.46), kind=kOutput, calls=%fused_computation.11 | convolution fusion | flops 1075838976 | bytes 5767168 | tf_op jit(solution)/shard_map/dot_general | solution.py:43
  168.7 7.4 %reshape.63 = bf16[32,512,128]{2,1,0:T(8,128)(2,1)} reshape(bf16[2048,1024]{1,0:T(8,128)(2,1)} %convolution_convert_fusion.2) | data formatting | bytes 8388608 | tf_op jit(solution)/shard_map/reshape | solution.py:44
  176.1 12.6 %psum.46 = f32[256]{0:T(256)S(1)} all-reduce(f32[256]{0:T(256)S(1)} %get-tuple-element.10), channel_id=1, replica_groups=mesh['crop'=4,'scene'=8] {'scene'}, use_global_device_ids=true, to_apply=%region_6.0 | all-reduce | flops 256 | bytes 2048 | tf_op jit(solution)/shard_map/psum | solution.py:101
  188.7 12.3 %psum.47 = f32[256]{0:T(256)S(1)} all-reduce(f32[256]{0:T(256)S(1)} %psum.46), channel_id=1, replica_groups=mesh['crop'=4,'scene'=8] {'crop'}, use_global_device_ids=true, to_apply=%region_7.0 | all-reduce | flops 256 | bytes 2048 | tf_op jit(solution)/shard_map/psum | solution.py:100
  201.0 0.6 broadcast_multiply_fusion.1
  201.6 4.9 %fusion.12 = bf16[32,192,128]{2,1,0:T(8,128)(2,1)} fusion(bf16[32,512,128]{2,1,0:T(8,128)(2,1)} %reshape.63, s32[32,192]{1,0:T(8,128)S(1)} %add.42), kind=kOutput, calls=%fused_computation.19 | convolution fusion | flops 809238528 | bytes 5791744 | tf_op jit(solution)/shard_map/brs,bsc->brc/dot_general | solution.py:45
  206.5 46.8 %all-reduce.7.cloned.1.call-done = (f32[1024,256]{1,0:T(8,128)}, f32[256,1024]{1,0:T(8,128)}) async-done(((f32[1024,256]{1,0:T(8,128)}, f32[256,1024]{1,0:T(8,128)}), (f32[1024,256]{1,0:T(8,128)}, f32[256,1024]{1,0:T(8,128)})) %all-reduce.7.cloned.1.call-update) | async-done | bytes 2097168 | tf_op jit(solution)/shard_map/psum | solution.py:100
  253.3 2.4 broadcast_multiply_fusion
  255.7 1.1 bitcast_bitcast_fusion
  (24 shorter events, 0.1 us)
Async XLA Ops:
  7.2 36.8 %copy-start = (bf16[1,6144,128]{2,1,0:T(8,128)(2,1)S(1)}, bf16[1,6144,128]{2,1,0:T(8,128)(2,1)}, u32[]{:S(2)}) copy-start(bf16[1,6144,128]{2,1,0:T(8,128)(2,1)} %param.10) | copy-start | bytes 4718596
  39.2 4.6 %copy-start.7 = (s32[1,6144]{1,0:T(1,128)S(1)}, s32[1,6144]{1,0:T(1,128)}, u32[]{:S(2)}) copy-start(s32[1,6144]{1,0:T(1,128)} %param.17) | copy-start | bytes 73732
  39.2 4.6 %copy-start.8 = (s32[1,6144]{1,0:T(1,128)S(1)}, s32[1,6144]{1,0:T(1,128)}, u32[]{:S(2)}) copy-start(s32[1,6144]{1,0:T(1,128)} %param.16) | copy-start | bytes 73732
  39.2 42.7 %all-to-all-start = ((bf16[8,8,64,256]{3,2,1,0:T(8,128)(2,1)}), bf16[8,8,64,256]{3,2,1,0:T(8,128)(2,1)}, u32[]{:S(2)}, u32[]{:S(2)}) async-start(bf16[8,8,64,256]{3,2,1,0:T(8,128)(2,1)} %bitcast.43), calls=%async_computation | async-start | bytes 4194304 | tf_op jit(solution)/shard_map/all_to_all | solution.py:89
  43.7 121.7 %all-reduce.5.cloned.1.call-start = ((), (), s32[]{:S(2)}) async-start(), calls=%async_computation.2 | async-start | bytes 4194304 | tf_op jit(solution)/shard_map/psum | solution.py:101
  51.0 7.3 %copy-start.6 = (bf16[8,256,128]{2,1,0:T(8,128)(2,1)S(1)}, bf16[8,256,128]{2,1,0:T(8,128)(2,1)}, u32[]{:S(2)}) copy-start(bf16[8,256,128]{2,1,0:T(8,128)(2,1)} %param.14) | copy-start | bytes 1572868
  66.7 7.4 %copy-start.9 = (s32[1,32,1]{1,2,0:T(1,128)S(1)}, s32[1,32,1]{1,2,0:T(1,128)}, u32[]{:S(2)}) copy-start(s32[1,32,1]{1,2,0:T(1,128)} %param.15) | copy-start | bytes 388
  90.6 4.9 %copy-start.2 = (bf16[2048,1024]{1,0:T(8,128)(2,1)S(1)}, bf16[2048,1024]{1,0:T(8,128)(2,1)}, u32[]{:S(2)}) copy-start(bf16[2048,1024]{1,0:T(8,128)(2,1)} %reshape.60) | copy-start | bytes 12582916
  90.6 4.9 %copy-start.3 = (f32[2048,256]{1,0:T(8,128)S(1)}, f32[2048,256]{1,0:T(8,128)}, u32[]{:S(2)}) copy-start(f32[2048,256]{1,0:T(8,128)} %reshape.69) | copy-start | bytes 6291460
  95.5 3.6 %copy-start.1 = (bf16[2048,1024]{1,0:T(8,128)(2,1)S(1)}, bf16[2048,1024]{1,0:T(8,128)(2,1)}, u32[]{:S(2)}) copy-start(bf16[2048,1024]{1,0:T(8,128)(2,1)} %reshape.65) | copy-start | bytes 12582916
  101.3 64.1 %copy-start.5 = (bf16[8,128,256]{2,1,0:T(8,128)(2,1)S(1)}, bf16[8,128,256]{2,1,0:T(8,128)(2,1)}, u32[]{:S(2)}) copy-start(bf16[8,128,256]{2,1,0:T(8,128)(2,1)} %param.13) | copy-start | bytes 1572868
  101.3 152.0 %all-reduce.7.cloned.1.call-start = ((), (), s32[]{:S(2)}) async-start(), calls=%async_computation.3 | async-start | bytes 4194304 | tf_op jit(solution)/shard_map/psum | solution.py:100
  253.3 2.4 copy-start.4
Sparse Core Ops, SparseCore 0:
  101.5 63.9 all-reduce.4
  167.8 85.4 all-reduce.6
